TPU v7x, 256 devices: a whole 4x4x8 slice. The times are simulated.
256 devices in a mesh: grp: 4 (over x), tok: 16 (over z, core), mdl: 4 (over y).
Axes of the slice: x: 4, y: 4, z: 8, core: 2. Of those that a mesh axis runs over, the one named last changes fastest.
Arguments:
- hidden_in: bfloat16 [4, 4096, 2048], P('grp', 'tok', 'mdl'), may hold values from -6 to 6
- suffix_len: int32 [4], P('grp'), may hold values from 512 to 4096, as said below
- norm_gain: bfloat16 [2048], replicated, may hold values from 0.099609375 to 1.8984375
- w_query: bfloat16 [2048, 2048], P(('grp', 'tok'), 'mdl'), may hold values from -0.5 to 0.5
- w_key: bfloat16 [2048, 512], P(('grp', 'tok'), 'mdl'), may hold values from -0.5 to 0.5
- w_value: bfloat16 [2048, 512], P(('grp', 'tok'), 'mdl'), may hold values from -0.125 to 0.125
- w_out: bfloat16 [2048, 2048], P(('grp', 'tok'), 'mdl'), may hold values from -0.5 to 0.5
- sink_logits: float32 [32], P('mdl'), may hold values from 8 to 12
- prefix_keys: bfloat16 [4, 4096, 512], P('grp', 'tok', 'mdl'), may hold values from -280 to 280
- prefix_values: bfloat16 [4, 4096, 512], P('grp', 'tok', 'mdl'), may hold values from -6 to 6
Outputs:
- attn_out: bfloat16 [4, 4096, 2048], P('grp', 'tok', 'mdl')
Inputs may be any that keep to these rules, and one draw needn't show every extreme that they name: `suffix_len`: one group in every draw has all 4096 slots live.
All inputs are finite; a program needn't handle non-finite values.
Results may differ from a plain program's by a relative error of at most 0.015.
The roundings to bfloat16 on the way count: a program that leaves them out, or rounds other values in their place, can miss the bound.
Values may be sent and summed in bfloat16 or wider, within the bound.
No kernel may reach another device: no remote copies, remote signals or barrier semaphores. Data moves between devices by JAX's collectives and lax.ppermute only.
A program may use at most 64 MiB of HBM per device.

v0:
```python
import jax
import jax.numpy as jnp
from jax import lax
from jax.sharding import PartitionSpec as P

HD = 64
SCORE_SCALE = 0.015625
EPSILON = 1e-05
LOG_THETA = 16.11809565095832


def rotate(heads_in, positions):
    half_dim = heads_in.shape[-1] // 2
    frequency = jnp.exp(
        -LOG_THETA * 2.0 * jnp.arange(half_dim, dtype=jnp.float32) / heads_in.shape[-1]
    )
    angles = positions[:, None] * frequency[None, :]
    cosine = jnp.concatenate([jnp.cos(angles), jnp.cos(angles)], axis=-1)[:, None, :]
    sine_part = jnp.concatenate([jnp.sin(angles), jnp.sin(angles)], axis=-1)[:, None, :]
    turned = jnp.concatenate([-heads_in[..., half_dim:], heads_in[..., :half_dim]], axis=-1)
    return heads_in * cosine + turned * sine_part


def on_device(
    hidden_in,
    suffix_len,
    norm_gain,
    w_query,
    w_key,
    w_value,
    w_out,
    sink_logits,
    prefix_keys,
    prefix_values,
):
    group_count, tok_rows, _ = hidden_in.shape
    head_count = sink_logits.shape[0]
    kv_width = prefix_keys.shape[2]
    kv_heads = kv_width // HD
    repeat = head_count // kv_heads
    tok_count = lax.axis_size("tok")
    own_index = lax.axis_index("tok")
    seq_span = tok_rows * tok_count
    gathered = lax.all_gather(hidden_in, "mdl", axis=2, tiled=True)
    features = gathered.astype(jnp.float32)
    normed = (
        features
        * lax.rsqrt(jnp.mean(features * features, axis=-1, keepdims=True) + EPSILON)
        * norm_gain.astype(jnp.float32)
    ).astype(jnp.bfloat16)
    normed = normed.reshape(group_count * tok_rows, -1)
    shard_rows = (
        lax.all_gather(w_query, ("grp", "tok"), axis=0, tiled=True),
        lax.all_gather(w_key, ("grp", "tok"), axis=0, tiled=True),
        lax.all_gather(w_value, ("grp", "tok"), axis=0, tiled=True),
    )
    query_sums, key_sums, value_sums = tuple(
        (
            jnp.dot(normed, weight_rows, preferred_element_type=jnp.float32)
            for weight_rows in shard_rows
        )
    )
    local_slots = own_index * tok_rows + jnp.arange(tok_rows, dtype=jnp.int32)
    query_pos = seq_span + local_slots
    positions = query_pos.astype(jnp.float32)
    queries = rotate(query_sums.reshape(group_count, tok_rows, head_count, HD), positions).astype(
        jnp.bfloat16
    )
    query_groups = queries.reshape(group_count, tok_rows, kv_heads, repeat, HD)
    new_keys = rotate(key_sums.reshape(group_count, tok_rows, kv_heads, HD), positions).astype(
        jnp.bfloat16
    )
    new_values = value_sums.astype(jnp.bfloat16).reshape(group_count, tok_rows, kv_width)
    kv_new = jnp.concatenate(
        [new_keys.reshape(group_count, tok_rows, kv_width), new_values], axis=2
    )
    kv_prefix = jnp.concatenate([prefix_keys, prefix_values], axis=2)

    def attend_part(softmax_state, key_block, key_pos):
        row_top, denoms, weighted = softmax_state
        key_count = key_block.shape[1]
        key_rows = key_block[..., :kv_width].reshape(group_count, key_count, kv_heads, HD)
        value_rows = key_block[..., kv_width:].reshape(group_count, key_count, kv_heads, HD)
        scores = (
            jnp.einsum(
                "gbkrh,gskh->gkrbs", query_groups, key_rows, preferred_element_type=jnp.float32
            )
            * SCORE_SCALE
        )
        allowed = (key_pos[None, :] <= query_pos[:, None]) & (
            key_pos[None, :] > query_pos[:, None] - seq_span
        )
        scores = jnp.where(allowed, scores, -jnp.inf)
        new_top = jnp.maximum(row_top, jnp.max(scores, axis=-1))
        expo_terms = jnp.where(allowed, jnp.exp(scores - new_top[..., None]), 0.0)
        rescale = jnp.exp(row_top - new_top)
        denoms = denoms * rescale + jnp.sum(expo_terms, axis=-1)
        weighted = weighted * rescale[..., None] + jnp.einsum(
            "gkrbs,gskh->gkrbh",
            expo_terms.astype(jnp.bfloat16),
            value_rows,
            preferred_element_type=jnp.float32,
        )
        return (new_top, denoms, weighted)

    def attend(softmax_state, key_block, key_pos):
        key_count = key_block.shape[1]
        block_count = key_count // 512
        blocks = jnp.swapaxes(
            key_block.reshape(group_count, block_count, 512, key_block.shape[2]), 0, 1
        )
        block_pos = key_pos.reshape(block_count, 512)

        def scan_step(inner_state, inputs):
            return (attend_part(inner_state, inputs[0], inputs[1]), None)

        final_state, _ = lax.scan(scan_step, softmax_state, (blocks, block_pos))
        return final_state

    sinks = sink_logits.reshape(1, kv_heads, repeat, 1)
    state_shape = (group_count, kv_heads, repeat, tok_rows)
    initial_state = (
        jnp.broadcast_to(sinks, state_shape),
        jnp.ones(state_shape, jnp.float32),
        jnp.zeros(state_shape + (HD,), jnp.float32),
    )
    softmax_state = initial_state
    shard_pair = (
        lax.all_gather(kv_prefix, "tok", axis=1, tiled=True),
        lax.all_gather(kv_new, "tok", axis=1, tiled=True),
    )
    row_count = shard_pair[0].shape[1]
    offsets = jnp.arange(row_count, dtype=jnp.int32)
    softmax_state = attend(softmax_state, shard_pair[0], offsets)
    final_state = attend(softmax_state, shard_pair[1], seq_span + offsets)
    row_top, denoms, weighted = final_state
    mixed = weighted / denoms[..., None]
    mixed = jnp.transpose(mixed, (0, 3, 1, 2, 4)).reshape(group_count, tok_rows, head_count * HD)
    live = local_slots[None, :] < suffix_len[:, None]
    mixed = jnp.where(live[..., None], mixed, 0.0).astype(jnp.bfloat16)
    mixed_rows = mixed.reshape(group_count * tok_rows, head_count * HD)
    partial_out = lax.dot_general(
        mixed_rows,
        lax.all_gather(w_out, ("grp", "tok"), axis=0, tiled=True),
        (((1,), (1,)), ((), ())),
        preferred_element_type=jnp.float32,
    )
    partial_out = partial_out.reshape(group_count, tok_rows, -1)
    summed = lax.psum_scatter(
        partial_out.astype(jnp.bfloat16), "mdl", scatter_dimension=2, tiled=True
    )
    return summed


def solution(mesh):
    placed = (
        P("grp", "tok", "mdl"),
        P("grp"),
        P(),
        P(("grp", "tok"), "mdl"),
        P(("grp", "tok"), "mdl"),
        P(("grp", "tok"), "mdl"),
        P(("grp", "tok"), "mdl"),
        P("mdl"),
        P("grp", "tok", "mdl"),
        P("grp", "tok", "mdl"),
    )
    return jax.shard_map(
        on_device, mesh=mesh, in_specs=placed, out_specs=P("grp", "tok", "mdl"), check_vma=False
    )
```

profile of v0, /device:TPU:2, one launch (start us, length us, event | category | flops | bytes accessed | tf_op | source)
XLA Modules:
  0.0 312.6 jit_solution(16367372434368591461)
XLA Ops:
  8.1 1.5 pad_maximum_fusion
  10.6 52.9 %all_gather.25 = bf16[2048,128]{1,0:T(8,128)(2,1)S(1)} all-gather(bf16[32,128]{1,0:T(8,128)(2,1)} %param.19), channel_id=1, replica_groups=mesh['grp'=4,'tok'=16,'mdl'=4] {'grp','tok'}, dimensions={0}, use_global_device_ids=true | all-gather | bytes 532480 | tf_op jit(solution)/shard_map/all_gather | solution.py:55
  63.5 48.3 %all_gather.24 = bf16[2048,128]{1,0:T(8,128)(2,1)S(1)} all-gather(bf16[32,128]{1,0:T(8,128)(2,1)} %param.18), channel_id=1, replica_groups=mesh['grp'=4,'tok'=16,'mdl'=4] {'grp','tok'}, dimensions={0}, use_global_device_ids=true | all-gather | bytes 532480 | tf_op jit(solution)/shard_map/all_gather | solution.py:54
  111.8 1.6 fusion.43
  113.4 1.8 fusion.55
  118.2 2.6 fusion.57
  121.0 37.4 %all-gather.6.cloned.1.call-done = bf16[1,4096,256]{2,1,0:T(8,128)(2,1)} async-done(((bf16[1,256,256]{2,1,0:T(8,128)(2,1)}), bf16[1,4096,256]{2,1,0:T(8,128)(2,1)}) %all-gather.6.cloned.1.call-update) | async-done | bytes 2097168 | tf_op jit(solution)/shard_map/all_gather | solution.py:129
  158.5 68.9 %while.35 = (s32[]{:T(128)}, f32[1,2,4,256]{3,2,1,0:T(4,128)S(1)}, f32[1,2,4,256]{3,2,1,0:T(4,128)S(1)}, f32[1,2,4,256,64]{3,4,2,1,0:T(8,128)S(1)}, s32[8,512]{1...) while((s32[]{:T(128)}, f32[1,2,4,256]{3,2,1,0:T(4,128)S(1)}, ...), condition=%wide.region_4.5_spmd.clone, body=%wide.region_1.4_spmd.clone.sunk | while | flops 282862080 | bytes 33171616 | solution.py:117
  160.7 1.9 copy-done
  163.7 3.4 %fusion.101 = f32[1,2,4,256,64]{3,4,2,1,0:T(8,128)S(1)} fusion(bf16[512,2,64,1]{0,2,3,1:T(8,128)(2,1)S(1)} %bitcast.229, f32[2,512,256,4]{2,1,3,0:T(8,128)} %copy-done, f32[2,4,256]{2,1,0:T(4,128)S(1)} %bitcast.228, pred[256,512]{0,1:T(8,128)(4,1)S(1)} %compare_and_fusion.5, f32[1,2,4,256,64]{3,4,2,1,0:T(8,128)S(1)} %get-tuple-element.487, ...), kind=kOutput, calls=%fused_computation.35.clone.1 | convolution fusion | flops 139853824 | bytes 5521409 | tf_op jit(solution)/shard_map/while/body/eval_jaxpr/gkrbs,gskh->gkrbh/dot_general | solution.py:98
  169.3 1.9 copy-done
  172.3 3.4 %fusion.101 = f32[1,2,4,256,64]{3,4,2,1,0:T(8,128)S(1)} fusion(bf16[512,2,64,1]{0,2,3,1:T(8,128)(2,1)S(1)} %bitcast.229, f32[2,512,256,4]{2,1,3,0:T(8,128)} %copy-done, f32[2,4,256]{2,1,0:T(4,128)S(1)} %bitcast.228, pred[256,512]{0,1:T(8,128)(4,1)S(1)} %compare_and_fusion.5, f32[1,2,4,256,64]{3,4,2,1,0:T(8,128)S(1)} %get-tuple-element.487, ...), kind=kOutput, calls=%fused_computation.35.clone.1 | convolution fusion | flops 139853824 | bytes 5521409 | tf_op jit(solution)/shard_map/while/body/eval_jaxpr/gkrbs,gskh->gkrbh/dot_general | solution.py:98
  177.9 1.9 copy-done
  180.9 3.4 %fusion.101 = f32[1,2,4,256,64]{3,4,2,1,0:T(8,128)S(1)} fusion(bf16[512,2,64,1]{0,2,3,1:T(8,128)(2,1)S(1)} %bitcast.229, f32[2,512,256,4]{2,1,3,0:T(8,128)} %copy-done, f32[2,4,256]{2,1,0:T(4,128)S(1)} %bitcast.228, pred[256,512]{0,1:T(8,128)(4,1)S(1)} %compare_and_fusion.5, f32[1,2,4,256,64]{3,4,2,1,0:T(8,128)S(1)} %get-tuple-element.487, ...), kind=kOutput, calls=%fused_computation.35.clone.1 | convolution fusion | flops 139853824 | bytes 5521409 | tf_op jit(solution)/shard_map/while/body/eval_jaxpr/gkrbs,gskh->gkrbh/dot_general | solution.py:98
  186.5 1.9 copy-done
  189.5 3.4 %fusion.101 = f32[1,2,4,256,64]{3,4,2,1,0:T(8,128)S(1)} fusion(bf16[512,2,64,1]{0,2,3,1:T(8,128)(2,1)S(1)} %bitcast.229, f32[2,512,256,4]{2,1,3,0:T(8,128)} %copy-done, f32[2,4,256]{2,1,0:T(4,128)S(1)} %bitcast.228, pred[256,512]{0,1:T(8,128)(4,1)S(1)} %compare_and_fusion.5, f32[1,2,4,256,64]{3,4,2,1,0:T(8,128)S(1)} %get-tuple-element.487, ...), kind=kOutput, calls=%fused_computation.35.clone.1 | convolution fusion | flops 139853824 | bytes 5521409 | tf_op jit(solution)/shard_map/while/body/eval_jaxpr/gkrbs,gskh->gkrbh/dot_general | solution.py:98
  195.2 1.9 copy-done
  198.1 3.4 %fusion.101 = f32[1,2,4,256,64]{3,4,2,1,0:T(8,128)S(1)} fusion(bf16[512,2,64,1]{0,2,3,1:T(8,128)(2,1)S(1)} %bitcast.229, f32[2,512,256,4]{2,1,3,0:T(8,128)} %copy-done, f32[2,4,256]{2,1,0:T(4,128)S(1)} %bitcast.228, pred[256,512]{0,1:T(8,128)(4,1)S(1)} %compare_and_fusion.5, f32[1,2,4,256,64]{3,4,2,1,0:T(8,128)S(1)} %get-tuple-element.487, ...), kind=kOutput, calls=%fused_computation.35.clone.1 | convolution fusion | flops 139853824 | bytes 5521409 | tf_op jit(solution)/shard_map/while/body/eval_jaxpr/gkrbs,gskh->gkrbh/dot_general | solution.py:98
  203.8 1.9 copy-done
  206.8 3.4 %fusion.101 = f32[1,2,4,256,64]{3,4,2,1,0:T(8,128)S(1)} fusion(bf16[512,2,64,1]{0,2,3,1:T(8,128)(2,1)S(1)} %bitcast.229, f32[2,512,256,4]{2,1,3,0:T(8,128)} %copy-done, f32[2,4,256]{2,1,0:T(4,128)S(1)} %bitcast.228, pred[256,512]{0,1:T(8,128)(4,1)S(1)} %compare_and_fusion.5, f32[1,2,4,256,64]{3,4,2,1,0:T(8,128)S(1)} %get-tuple-element.487, ...), kind=kOutput, calls=%fused_computation.35.clone.1 | convolution fusion | flops 139853824 | bytes 5521409 | tf_op jit(solution)/shard_map/while/body/eval_jaxpr/gkrbs,gskh->gkrbh/dot_general | solution.py:98
  212.4 1.9 copy-done
  215.4 3.4 %fusion.101 = f32[1,2,4,256,64]{3,4,2,1,0:T(8,128)S(1)} fusion(bf16[512,2,64,1]{0,2,3,1:T(8,128)(2,1)S(1)} %bitcast.229, f32[2,512,256,4]{2,1,3,0:T(8,128)} %copy-done, f32[2,4,256]{2,1,0:T(4,128)S(1)} %bitcast.228, pred[256,512]{0,1:T(8,128)(4,1)S(1)} %compare_and_fusion.5, f32[1,2,4,256,64]{3,4,2,1,0:T(8,128)S(1)} %get-tuple-element.487, ...), kind=kOutput, calls=%fused_computation.35.clone.1 | convolution fusion | flops 139853824 | bytes 5521409 | tf_op jit(solution)/shard_map/while/body/eval_jaxpr/gkrbs,gskh->gkrbh/dot_general | solution.py:98
  221.0 1.9 copy-done
  224.0 3.4 %fusion.101 = f32[1,2,4,256,64]{3,4,2,1,0:T(8,128)S(1)} fusion(bf16[512,2,64,1]{0,2,3,1:T(8,128)(2,1)S(1)} %bitcast.229, f32[2,512,256,4]{2,1,3,0:T(8,128)} %copy-done, f32[2,4,256]{2,1,0:T(4,128)S(1)} %bitcast.228, pred[256,512]{0,1:T(8,128)(4,1)S(1)} %compare_and_fusion.5, f32[1,2,4,256,64]{3,4,2,1,0:T(8,128)S(1)} %get-tuple-element.487, ...), kind=kOutput, calls=%fused_computation.35.clone.1 | convolution fusion | flops 139853824 | bytes 5521409 | tf_op jit(solution)/shard_map/while/body/eval_jaxpr/gkrbs,gskh->gkrbh/dot_general | solution.py:98
  227.5 1.8 copy.33
  229.2 27.5 %while.34 = (s32[]{:T(128)}, f32[1,2,4,256]{3,2,1,0:T(4,128)S(1)}, f32[1,2,4,256]{3,2,1,0:T(4,128)S(1)}, f32[1,2,4,256,64]{3,4,2,1,0:T(8,128)S(1)}, s32[8,512]{1...) while((s32[]{:T(128)}, f32[1,2,4,256]{3,2,1,0:T(4,128)S(1)}, ...), condition=%wide.region_8.9_spmd.clone, body=%wide.region_5.8_spmd.clone.sunk | while | flops 282728960 | bytes 15870065 | solution.py:117
  231.4 1.3 fusion.93
  238.3 1.3 fusion.93
  255.5 1.3 fusion.93
  256.9 20.7 %all-gather.14.cloned.1.call-done = bf16[2048,512]{1,0:T(8,128)(2,1)} async-done(((bf16[32,512]{1,0:T(8,128)(2,1)}), bf16[2048,512]{1,0:T(8,128)(2,1)}) %all-gather.14.cloned.1.call-update) | async-done | bytes 2097168 | tf_op jit(solution)/shard_map/all_gather | solution.py:144
  277.5 3.3 %fusion.42 = bf16[1,256,2048]{2,1,0:T(8,128)(2,1)} fusion(bf16[256,512]{0,1:T(8,128)(2,1)S(1)} %fusion.50, bf16[2048,512]{1,0:T(8,128)(2,1)} %all-gather.14.cloned.1.call-done), kind=kOutput, calls=%fused_computation.55 | convolution fusion | flops 537395200 | bytes 3407872 | tf_op jit(solution)/shard_map/dot_general | solution.py:142
  280.9 24.9 %reduce-scatter.2.cloned.1.call-done = bf16[1,256,512]{2,1,0:T(8,128)(2,1)} async-done(((bf16[1,256,2048]{2,1,0:T(8,128)(2,1)}), bf16[1,256,512]{2,1,0:T(8,128)(2,1)}) %reduce-scatter.2.cloned.1.call-update) | async-done | bytes 262160 | tf_op jit(solution)/shard_map/reduce_scatter | solution.py:149
  (222 shorter events, 53.6 us)
Async XLA Ops:
  6.5 105.2 %all-gather.8.cloned.1.call-start = ((), (), s32[]{:S(2)}) async-start(), calls=%async_computation.2 | async-start | bytes 1310720 | tf_op jit(solution)/shard_map/all_gather | solution.py:44
  7.3 111.0 %all-gather.10.cloned.1.call-start = ((), (), s32[]{:S(2)}) async-start(), calls=%async_computation.3 | async-start | bytes 2129920 | tf_op jit(solution)/shard_map/all_gather | solution.py:53
  8.0 150.4 %all-gather.6.cloned.1.call-start = ((), (), s32[]{:S(2)}) async-start(), calls=%async_computation.1 | async-start | bytes 2228224 | tf_op jit(solution)/shard_map/all_gather | solution.py:129
  9.6 107.8 %copy-start.2 = (f32[8]{0:T(128)S(1)}, f32[8]{0:T(128)}, u32[]{:S(2)}) copy-start(f32[8]{0:T(128)} %param.21) | copy-start | bytes 100
  9.6 217.8 %all-gather.12.cloned.1.call-start = ((), (), s32[]{:S(2)}) async-start(), calls=%async_computation.4 | async-start | bytes 2228224 | tf_op jit(solution)/shard_map/all_gather | solution.py:130
  111.8 3.5 %copy-start.1 = (bf16[1,256,2048]{2,1,0:T(8,128)(2,1)S(1)}, bf16[1,256,2048]{2,1,0:T(8,128)(2,1)}, u32[]{:S(2)}) copy-start(bf16[1,256,2048]{2,1,0:T(8,128)(2,1)} %all-gather.8.cloned.1.call-done) | copy-start | bytes 3145732
  116.5 161.0 %all-gather.14.cloned.1.call-start = ((), (), s32[]{:S(2)}) async-start(), calls=%async_computation.5 | async-start | bytes 2129920 | tf_op jit(solution)/shard_map/all_gather | solution.py:144
  117.1 188.7 %reduce-scatter.2.cloned.1.call-start = ((), (), s32[]{:S(2)}) async-start(), calls=%async_computation.6 | async-start | bytes 1310720 | tf_op jit(solution)/shard_map/reduce_scatter | solution.py:149
  160.7 2.0 copy-start
  169.3 2.0 copy-start
  177.9 2.0 copy-start
  186.5 2.0 copy-start
  195.1 2.0 copy-start
  203.8 2.0 copy-start
  212.4 2.0 copy-start
  221.0 2.0 copy-start
Sparse Core Ops, SparseCore 0:
  9.2 29.4 all-gather.7
  41.5 76.7 all-gather.9
  120.1 38.3 all-gather.5
  160.1 39.2 all-gather.11
  202.0 75.5 all-gather.13
  281.0 24.7 reduce-scatter.1
where the time goes:
time: 314 us; the launch traced here: 313 us
  blocking collectives  101 us (32%)
  waiting for transfers between devices  85.1 us (27%)
  matrix products  58.7 us (19%)
  local copies, waits for them, and re-layouts  27.1 us (9%)
  other arithmetic  24.6 us (8%)
  between operations  14.3 us (5%)
    all_gather x1, blocking collectives, on_device(): lax.all_gather(w_value, ('grp', 'tok'), axis=0, tiled=True)  52.9 us
    all_gather x1, blocking collectives, on_device(): lax.all_gather(w_key, ('grp', 'tok'), axis=0, tiled=True)  48.3 us
    all_gather x1, waiting for transfers between devices, on_device(): lax.all_gather(kv_prefix, 'tok', axis=1, tiled=True)  37.4 us
    dot_general x16, matrix products, attend_part(): jnp.einsum('gkrbs,gskh->gkrbh', expo_terms.astype(jnp.bfloat16), value_ro...  37.4 us
    reduce_scatter x1, waiting for transfers between devices, on_device(): lax.psum_scatter(partial_out.astype(jnp.bfloat16), 'mdl', scatter_dimensi...  24.9 us
    all_gather x1, waiting for transfers between devices, on_device(): lax.all_gather(w_out, ('grp', 'tok'), axis=0, tiled=True)  20.7 us
    reduce_sum x16, other arithmetic, attend_part(): denoms = denoms * rescale + jnp.sum(expo_terms, axis=-1)  16.2 us
    while x32, local copies, waits for them, and re-layouts  15.5 us
  transfers between devices with their start and end apart: 6, of which 4 were waited for; matrix products, arithmetic and copies ran while one was open for 29% of the time, Pallas kernels for 0%

commit v1 on v0

--- a/solution.py
+++ b/solution.py
@@ -2,11 +2,23 @@
 import jax.numpy as jnp
 from jax import lax
 from jax.sharding import PartitionSpec as P
+from jax.lax import all_to_all, axis_size
 
 HD = 64
 SCORE_SCALE = 0.015625
 EPSILON = 1e-05
 LOG_THETA = 16.11809565095832
+
+
+def forms_solve(matrix):
+    wide_n = axis_size("tok")
+    return all_to_all(
+        jnp.tile(matrix, list(map(lambda w: wide_n if w == 1 else 1, range(matrix.ndim)))),
+        concat_axis=1,
+        tiled=True,
+        split_axis=1,
+        axis_name="tok",
+    )
 
 
 def rotate(heads_in, positions):
@@ -125,10 +137,7 @@
         jnp.zeros(state_shape + (HD,), jnp.float32),
     )
     softmax_state = initial_state
-    shard_pair = (
-        lax.all_gather(kv_prefix, "tok", axis=1, tiled=True),
-        lax.all_gather(kv_new, "tok", axis=1, tiled=True),
-    )
+    shard_pair = (forms_solve(kv_prefix), lax.all_gather(kv_new, "tok", axis=1, tiled=True))
     row_count = shard_pair[0].shape[1]
     offsets = jnp.arange(row_count, dtype=jnp.int32)
     softmax_state = attend(softmax_state, shard_pair[0], offsets)

time: 314 us -> 373 us (1.19)
  local copies, waits for them, and re-layouts: 27.1 us -> 53.2 us
  other arithmetic: 24.6 us -> 46.3 us
  matrix products: 58.7 us -> 75.9 us
  waiting for transfers between devices: 85.1 us -> 74.3 us
  starting transfers between devices: 0.38 us -> 4.99 us
    all_to_all x0 -> x1, waiting for transfers between devices: none -> 47.1 us  [forms_solve(): all_to_all(jnp.tile(matrix, list(map(lambda w: wide_n if w == 1 else 1, r...]
    all_gather x1 -> x0, waiting for transfers between devices: 37.4 us -> none  [on_device(): lax.all_gather(kv_prefix, 'tok', axis=1, tiled=True)]
    another operation x0 -> x2, local copies, waits for them, and re-layouts: none -> 25.2 us  [forms_solve(): jnp.tile(matrix, list(map(lambda w: wide_n if w == 1 else 1, range(matrix...]
    unnamed x2 -> x3, other arithmetic: 0.01 us -> 21.6 us
    all_gather x1, waiting for transfers between devices: 20.7 us -> 0.02 us  [on_device(): lax.all_gather(w_out, ('grp', 'tok'), axis=0, tiled=True)]
    dot_general x16, matrix products: 13 us -> 28.6 us  [attend_part(): jnp.einsum('gbkrh,gskh->gkrbs', query_groups, key_rows, preferred_element...]
    while x32 -> x64, local copies, waits for them, and re-layouts: 15.5 us -> 0.14 us
    unnamed x4 -> x16, local copies, waits for them, and re-layouts: 0.01 us -> 11.9 us
  transfers between devices with their start and end apart: 6 -> 6, of which waited for: 4 -> 2; matrix products, arithmetic and copies ran while one was open for 29% -> 46% of each run, Pallas kernels for 0% -> 0%
where the time goes in v1:
time: 373 us; the launch traced here: 372 us
  blocking collectives  101 us (27%)
  matrix products  75.9 us (20%)
  waiting for transfers between devices  74.3 us (20%)
  local copies, waits for them, and re-layouts  53.2 us (14%)
  other arithmetic  46.3 us (12%)
  between operations  14.1 us (4%)
  starting transfers between devices  4.99 us (1%)
    all_gather x1, blocking collectives, on_device(): lax.all_gather(w_key, ('grp', 'tok'), axis=0, tiled=True)  52.9 us
    all_gather x1, blocking collectives, on_device(): lax.all_gather(w_value, ('grp', 'tok'), axis=0, tiled=True)  48.5 us
    all_to_all x1, waiting for transfers between devices, forms_solve(): all_to_all(jnp.tile(matrix, list(map(lambda w: wide_n if w == 1 else 1, r...  47.1 us
    dot_general x16, matrix products, attend_part(): jnp.einsum('gkrbs,gskh->gkrbh', expo_terms.astype(jnp.bfloat16), value_ro...  38.6 us
    dot_general x16, matrix products, attend_part(): jnp.einsum('gbkrh,gskh->gkrbs', query_groups, key_rows, preferred_element...  28.6 us
    another operation x2, local copies, waits for them, and re-layouts, forms_solve(): jnp.tile(matrix, list(map(lambda w: wide_n if w == 1 else 1, range(matrix...  25.2 us
    reduce_scatter x1, waiting for transfers between devices, on_device(): lax.psum_scatter(partial_out.astype(jnp.bfloat16), 'mdl', scatter_dimensi...  25.1 us
    unnamed x3, other arithmetic  21.6 us
  transfers between devices with their start and end apart: 6, of which 2 were waited for; matrix products, arithmetic and copies ran while one was open for 46% of the time, Pallas kernels for 0%

profile of v1, /device:TPU:2, one launch (start us, length us, event | category | flops | bytes accessed | tf_op | source)
XLA Modules:
  0.0 371.5 jit_solution(14840170086851981876)
XLA Ops:
  9.0 52.9 %all_gather.20 = bf16[2048,128]{1,0:T(8,128)(2,1)S(1)} all-gather(bf16[32,128]{1,0:T(8,128)(2,1)} %param.18), channel_id=1, replica_groups=mesh['grp'=4,'tok'=16,'mdl'=4] {'grp','tok'}, dimensions={0}, use_global_device_ids=true | all-gather | bytes 532480 | tf_op jit(solution)/shard_map/all_gather | solution.py:66
  61.9 48.5 %all_gather.21 = bf16[2048,128]{1,0:T(8,128)(2,1)S(1)} all-gather(bf16[32,128]{1,0:T(8,128)(2,1)} %param.19), channel_id=1, replica_groups=mesh['grp'=4,'tok'=16,'mdl'=4] {'grp','tok'}, dimensions={0}, use_global_device_ids=true | all-gather | bytes 532480 | tf_op jit(solution)/shard_map/all_gather | solution.py:67
  111.9 1.8 fusion.55
  115.3 25.0 %copy.49 = bf16[1,4096,256]{2,0,1:T(2,128)(2,1)} copy(bf16[1,4096,256]{2,1,0:T(8,128)(2,1)S(1)} %bitcast.233) | data formatting | bytes 4194304 | tf_op jit(solution)/shard_map/tile | solution.py:16
  140.9 21.6 %reduce.17 = bf16[4096,256]{1,0:T(8,128)(2,1)S(1)} reduce(bf16[4096,1,256]{2,1,0:T(2,128)(2,1)} %bitcast.229, bf16[]{:T(256)} %broadcast.177), dimensions={1}, to_apply=%bitcast.166.reduce_sub_computation | reduce | bytes 4194306
  162.5 2.1 reshape.352
  164.6 4.6 %all-to-all-start = ((bf16[16,2,32768]{2,1,0:T(2,128)(2,1)}), bf16[16,2,32768]{2,1,0:T(2,128)(2,1)S(1)}, u32[]{:S(2)}, u32[]{:S(2)}) async-start(bf16[16,2,32768]{2,1,0:T(2,128)(2,1)} %reshape.352), calls=%async_computation | async-start | bytes 4194304 | tf_op jit(solution)/shard_map/all_to_all | solution.py:15
  172.5 47.1 %all-to-all-done = bf16[16,2,32768]{2,1,0:T(2,128)(2,1)S(1)} async-done(((bf16[16,2,32768]{2,1,0:T(2,128)(2,1)}), bf16[16,2,32768]{2,1,0:T(2,128)(2,1)S(1)}, u32[]{:S(2)}, u32[]{:S(2)}) %all-to-all-start) | async-done | bytes 2097184 | tf_op jit(solution)/shard_map/all_to_all | solution.py:15
  219.6 6.7 %reshape.353 = bf16[4096,1,256]{2,1,0:T(2,128)(2,1)} reshape(bf16[16,2,32768]{2,1,0:T(2,128)(2,1)S(1)} %all-to-all-done) | data formatting | bytes 4194304
  226.4 2.5 copy.44
  228.9 2.9 fusion.57
  232.1 69.1 %while.35 = (s32[]{:T(128)}, f32[1,2,4,256]{3,2,1,0:T(4,128)S(1)}, f32[1,2,4,256]{3,2,1,0:T(4,128)S(1)}, f32[1,2,4,256,64]{3,4,2,1,0:T(8,128)}, s32[8,512]{1,0:T...) while((s32[]{:T(128)}, f32[1,2,4,256]{3,2,1,0:T(4,128)S(1)}, ...), condition=%wide.region_4.5_spmd.clone, body=%wide.region_1.4_spmd.clone.sunk | while | flops 282862080 | bytes 37365964 | solution.py:129
  233.3 2.8 fusion.98
  236.1 3.5 fusion.101
  241.9 2.8 fusion.98
  244.7 3.5 fusion.101
  250.6 2.8 fusion.98
  253.4 3.6 fusion.101
  259.2 2.8 fusion.98
  262.0 3.6 fusion.101
  267.8 2.8 fusion.98
  270.7 3.5 fusion.101
  276.5 2.8 fusion.98
  279.3 3.5 fusion.101
  285.1 2.8 fusion.98
  287.9 3.5 fusion.101
  293.8 2.8 fusion.98
  296.6 3.5 fusion.101
  301.2 1.8 copy.48
  303.1 33.2 %while.34 = (s32[]{:T(128)}, f32[1,2,4,256]{3,2,1,0:T(4,128)S(1)}, f32[1,2,4,256]{3,2,1,0:T(4,128)S(1)}, f32[1,2,4,256,64]{3,4,2,1,0:T(8,128)S(1)}, s32[8,512]{1...) while((s32[]{:T(128)}, f32[1,2,4,256]{3,2,1,0:T(4,128)S(1)}, ...), condition=%wide.region_8.9_spmd.clone, body=%wide.region_5.8_spmd.clone.sunk | while | flops 282728960 | bytes 15870057 | solution.py:129
  336.5 3.3 fusion.42
  339.8 25.1 %reduce-scatter.2.cloned.1.call-done = bf16[1,256,512]{2,1,0:T(8,128)(2,1)} async-done(((bf16[1,256,2048]{2,1,0:T(8,128)(2,1)}), bf16[1,256,512]{2,1,0:T(8,128)(2,1)}) %reduce-scatter.2.cloned.1.call-update) | async-done | bytes 262160 | tf_op jit(solution)/shard_map/reduce_scatter | solution.py:158
  (268 shorter events, 59.5 us)
Async XLA Ops:
  6.5 103.8 %all-gather.5.cloned.1.call-start = ((), (), s32[]{:S(2)}) async-start(), calls=%async_computation.2 | async-start | bytes 1310720 | tf_op jit(solution)/shard_map/all_gather | solution.py:56
  7.3 107.8 %copy-start.5 = (bf16[1,256,128]{2,1,0:T(8,128)(2,1)S(1)}, bf16[1,256,128]{2,1,0:T(8,128)(2,1)}, u32[]{:S(2)}) copy-start(bf16[1,256,128]{2,1,0:T(8,128)(2,1)} %param.23) | copy-start | bytes 196612
  7.3 107.8 %copy-start.6 = (bf16[1,256,128]{2,1,0:T(8,128)(2,1)S(1)}, bf16[1,256,128]{2,1,0:T(8,128)(2,1)}, u32[]{:S(2)}) copy-start(bf16[1,256,128]{2,1,0:T(8,128)(2,1)} %param.22) | copy-start | bytes 196612
  7.3 221.7 %all-gather.7.cloned.1.call-start = ((), (), s32[]{:S(2)}) async-start(), calls=%async_computation.3 | async-start | bytes 2129920 | tf_op jit(solution)/shard_map/all_gather | solution.py:65
  8.0 293.2 %all-gather.9.cloned.1.call-start = ((), (), s32[]{:S(2)}) async-start(), calls=%async_computation.4 | async-start | bytes 2228224 | tf_op jit(solution)/shard_map/all_gather | solution.py:140
  110.3 3.5 copy-start.1
  162.5 7.6 %copy-start.8 = (f32[8]{0:T(128)S(1)}, f32[8]{0:T(128)}, u32[]{:S(2)}) copy-start(f32[8]{0:T(128)} %param.21) | copy-start | bytes 100
  164.6 55.1 %all-to-all-start = ((bf16[16,2,32768]{2,1,0:T(2,128)(2,1)}), bf16[16,2,32768]{2,1,0:T(2,128)(2,1)S(1)}, u32[]{:S(2)}, u32[]{:S(2)}) async-start(bf16[16,2,32768]{2,1,0:T(2,128)(2,1)} %reshape.352), calls=%async_computation | async-start | bytes 4194304 | tf_op jit(solution)/shard_map/all_to_all | solution.py:15
  169.2 167.3 %all-gather.11.cloned.1.call-start = ((), (), s32[]{:S(2)}) async-start(), calls=%async_computation.5 | async-start | bytes 2129920 | tf_op jit(solution)/shard_map/all_gather | solution.py:153
  169.8 195.2 %reduce-scatter.2.cloned.1.call-start = ((), (), s32[]{:S(2)}) async-start(), calls=%async_computation.6 | async-start | bytes 1310720 | tf_op jit(solution)/shard_map/reduce_scatter | solution.py:158
  232.1 4.0 %copy-start.2 = (f32[1,2,4,256,64]{3,4,2,1,0:T(8,128)S(1)}, f32[1,2,4,256,64]{3,4,2,1,0:T(8,128)}, u32[]{:S(2)}) copy-start(f32[1,2,4,256,64]{3,4,2,1,0:T(8,128)} %get-tuple-element.519) | copy-start | bytes 1572868 | tf_op jit(solution)/shard_map/while
  236.1 3.6 copy-start
  240.7 4.0 %copy-start.2 = (f32[1,2,4,256,64]{3,4,2,1,0:T(8,128)S(1)}, f32[1,2,4,256,64]{3,4,2,1,0:T(8,128)}, u32[]{:S(2)}) copy-start(f32[1,2,4,256,64]{3,4,2,1,0:T(8,128)} %get-tuple-element.519) | copy-start | bytes 1572868 | tf_op jit(solution)/shard_map/while
  244.7 3.6 copy-start
  248.3 1.1 copy-start.3
  249.4 4.0 %copy-start.2 = (f32[1,2,4,256,64]{3,4,2,1,0:T(8,128)S(1)}, f32[1,2,4,256,64]{3,4,2,1,0:T(8,128)}, u32[]{:S(2)}) copy-start(f32[1,2,4,256,64]{3,4,2,1,0:T(8,128)} %get-tuple-element.519) | copy-start | bytes 1572868 | tf_op jit(solution)/shard_map/while
  253.3 3.6 copy-start
  256.9 1.1 copy-start.3
  258.0 4.0 %copy-start.2 = (f32[1,2,4,256,64]{3,4,2,1,0:T(8,128)S(1)}, f32[1,2,4,256,64]{3,4,2,1,0:T(8,128)}, u32[]{:S(2)}) copy-start(f32[1,2,4,256,64]{3,4,2,1,0:T(8,128)} %get-tuple-element.519) | copy-start | bytes 1572868 | tf_op jit(solution)/shard_map/while
  262.0 3.6 copy-start
  265.6 1.1 copy-start.3
  266.7 4.0 %copy-start.2 = (f32[1,2,4,256,64]{3,4,2,1,0:T(8,128)S(1)}, f32[1,2,4,256,64]{3,4,2,1,0:T(8,128)}, u32[]{:S(2)}) copy-start(f32[1,2,4,256,64]{3,4,2,1,0:T(8,128)} %get-tuple-element.519) | copy-start | bytes 1572868 | tf_op jit(solution)/shard_map/while
  270.6 3.6 copy-start
  274.2 1.1 copy-start.3
  275.3 4.0 %copy-start.2 = (f32[1,2,4,256,64]{3,4,2,1,0:T(8,128)S(1)}, f32[1,2,4,256,64]{3,4,2,1,0:T(8,128)}, u32[]{:S(2)}) copy-start(f32[1,2,4,256,64]{3,4,2,1,0:T(8,128)} %get-tuple-element.519) | copy-start | bytes 1572868 | tf_op jit(solution)/shard_map/while
  279.3 3.6 copy-start
  283.9 4.0 %copy-start.2 = (f32[1,2,4,256,64]{3,4,2,1,0:T(8,128)S(1)}, f32[1,2,4,256,64]{3,4,2,1,0:T(8,128)}, u32[]{:S(2)}) copy-start(f32[1,2,4,256,64]{3,4,2,1,0:T(8,128)} %get-tuple-element.519) | copy-start | bytes 1572868 | tf_op jit(solution)/shard_map/while
  287.9 3.6 copy-start
  292.6 4.0 %copy-start.2 = (f32[1,2,4,256,64]{3,4,2,1,0:T(8,128)S(1)}, f32[1,2,4,256,64]{3,4,2,1,0:T(8,128)}, u32[]{:S(2)}) copy-start(f32[1,2,4,256,64]{3,4,2,1,0:T(8,128)} %get-tuple-element.519) | copy-start | bytes 1572868 | tf_op jit(solution)/shard_map/while
  296.5 3.6 copy-start
  301.2 1.9 copy-start.4
  303.1 33.3 %copy-start.7 = (pred[256]{0:T(512)(128)(4,1)S(1)}, pred[256]{0:T(512)(128)(4,1)}, u32[]{:S(2)}) copy-start(pred[256]{0:T(512)(128)(4,1)} %fusion.53) | copy-start | bytes 772
  (4 other events, 4.3 us)
Sparse Core Ops, SparseCore 0:
  9.2 29.4 all-gather.4
  41.5 76.6 all-gather.6
  119.9 39.5 all-gather.8
  172.5 91.1 all-gather.10
  340.0 24.9 reduce-scatter.1
